TPU v7x, 512 devices: a whole 4x4x16 slice. The times are simulated.
512 devices in a mesh: case: 32 (over z, x_hi), bx: 8 (over x_lo, y), by: 2 (over core).
Axes of the slice: x: 4 (x_hi: 2, x_lo: 2; x = x_hi * 2 + x_lo), y: 4, z: 16, core: 2. Of those that a mesh axis runs over, the one named last changes fastest.
Arguments:
- displacements: bfloat16 [64, 3, 64, 16, 256], P('case', None, 'bx', 'by'), may hold values from -6 to 6
- material_ids: int32 [64, 16, 256], P('bx', 'by'), may hold values from 0 to 7
- lame: float32 [2, 8], replicated, may hold values from 0.5 to 2
- slab_bounds: int32 [2, 64], P(None, 'bx'), may hold values from 0 to 256, as said below
- load_history: bfloat16 [1024, 64], replicated, may hold values from -0.75 to 0.75
Outputs:
- vm_peak: float32 [64, 16, 256], P('bx', 'by', 'case')
- hyd_range: float32 [64, 16, 256], P('bx', 'by', 'case')
Inputs may be any that keep to these rules, and one draw needn't show every extreme that they name: `slab_bounds`: row 0 lies below 64 and row 1 above 192 for every x.
All inputs are finite; a program needn't handle non-finite values.
Results may differ from a plain program's by a relative error of at most 0.00097.
Values may be sent and summed in bfloat16 or wider, within the bound.
A program may use at most 64 MiB of HBM per device.

v0:
```python
import jax
import jax.numpy as jnp
from jax import lax
from jax.sharding import PartitionSpec as P


def with_halo(shard, sides, width):
    edges = {}
    for axis, dim in sides:
        devices, length = (lax.axis_size(axis), shard.shape[dim])
        up = [(i, (i + 1) % devices) for i in range(devices - 1)]
        last = lax.slice_in_dim(shard, length - width, length, axis=dim)
        leading = lax.slice_in_dim(shard, 0, width, axis=dim)
        edges[dim] = (
            lax.ppermute(last, axis, up),
            lax.ppermute(leading, axis, [(b, a) for a, b in up]),
        )
    done = []
    for _, dim in sides:
        low, high = edges[dim]
        around = [(width, width) if d in done else (0, 0) for d in range(shard.ndim)]
        shard = jnp.concatenate([jnp.pad(low, around), shard, jnp.pad(high, around)], axis=dim)
        done.append(dim)
    return shard


def combine_stress(grads, shear_mod, lame_first, weight):
    trace = grads[0][0] + grads[1][1] + grads[2][2]
    normal_x = (lame_first * trace + 2.0 * shear_mod * grads[0][0]) * weight
    normal_y = (lame_first * trace + 2.0 * shear_mod * grads[1][1]) * weight
    normal_z = (lame_first * trace + 2.0 * shear_mod * grads[2][2]) * weight
    shear_xy = shear_mod * (grads[0][1] + grads[1][0]) * weight
    shear_yz = shear_mod * (grads[1][2] + grads[2][1]) * weight
    shear_zx = shear_mod * (grads[2][0] + grads[0][2]) * weight
    return jnp.stack([normal_x, normal_y, normal_z, shear_xy, shear_yz, shear_zx], axis=-4)


def flat_derivative(field, along, width):
    total = field.shape[-1]
    if along == 0:
        return 0.5 * (field[..., 1:-1, 2 * width :] - field[..., 1:-1, : total - 2 * width])
    if along == 1:
        return 0.5 * (
            field[..., 1:-1, width + 1 : total - width + 1]
            - field[..., 1:-1, width - 1 : total - width - 1]
        )
    return 0.5 * (field[..., 2:, width : total - width] - field[..., :-2, width : total - width])


def flat_stress(local_field, shear_mod, lame_first, weight, width):
    local_field = local_field.astype(jnp.float32)
    grads = [
        [flat_derivative(local_field[:, comp], along, width) for along in range(3)]
        for comp in range(3)
    ]
    stacked = combine_stress(grads, shear_mod, lame_first, weight)
    return jnp.moveaxis(stacked, 0, 1)


def flat_layout(values, slab):
    padded = jnp.pad(values, ((0, 0), (1, 1), (0, 0)))
    return jnp.transpose(padded, (2, 0, 1)).reshape(slab, -1)


def material_moduli(material_ids, lame):
    shear_mod = jnp.zeros(material_ids.shape, jnp.float32)
    lame_first = jnp.zeros(material_ids.shape, jnp.float32)
    for material in range(lame.shape[1]):
        picked = material_ids == material
        shear_mod = jnp.where(picked, lame[0, material], shear_mod)
        lame_first = jnp.where(picked, lame[1, material], lame_first)
    return (shear_mod, lame_first)


def histories(load_history, blocks):
    cases, comps, rows, cols, single, slab = blocks.shape
    flat = blocks.reshape(cases, comps * rows * cols * single * slab)
    total = load_history.shape[0]
    step_len = min(128, total)
    top_mises = None
    for begin in range(0, total, step_len):
        factors = load_history[begin : begin + step_len]
        history = jnp.dot(factors, flat, preferred_element_type=jnp.float32).reshape(
            step_len, comps, -1
        )
        diff_one = history[:, 0] - history[:, 1]
        diff_two = history[:, 1] - history[:, 2]
        diff_three = history[:, 2] - history[:, 0]
        mises2 = 0.5 * (diff_one * diff_one + diff_two * diff_two + diff_three * diff_three)
        mises2 = mises2 + 3.0 * (
            history[:, 3] * history[:, 3]
            + history[:, 4] * history[:, 4]
            + history[:, 5] * history[:, 5]
        )
        hydro = (history[:, 0] + history[:, 1] + history[:, 2]) / 3.0
        block_mises = jnp.max(mises2, axis=0)
        block_high = jnp.max(hydro, axis=0)
        block_low = jnp.min(hydro, axis=0)
        if top_mises is None:
            top_mises, high, low = (block_mises, block_high, block_low)
        else:
            top_mises = jnp.maximum(top_mises, block_mises)
            high = jnp.maximum(high, block_high)
            low = jnp.minimum(low, block_low)
    peak = jnp.sqrt(top_mises).reshape(rows, cols, slab)
    spread = (high - low).reshape(rows, cols, slab)
    return (peak, spread)


def shards(displacements, material_ids, lame, slab_bounds, load_history):
    cases_here = displacements.shape[0]
    rows = displacements.shape[2]
    cols = displacements.shape[3]
    depth = displacements.shape[4]
    groups = lax.axis_size("case")
    slab = depth // groups
    shear_mod, lame_first = material_moduli(material_ids, lame)
    levels = jnp.arange(depth, dtype=jnp.int32)
    inside = (slab_bounds[0][:, None] <= levels[None, :]) & (
        levels[None, :] < slab_bounds[1][:, None]
    )
    weight = inside.astype(jnp.float32)[:, None, :]
    bordered = with_halo(displacements, (("bx", 2), ("by", 3)), 1)
    extended = jnp.pad(bordered, ((0, 0), (0, 0), (0, 0), (0, 0), (1, 1)))
    width = cols + 2
    plane = (rows + 2) * width
    planes = jnp.transpose(extended, (0, 1, 4, 2, 3)).reshape(cases_here, 3, depth + 2, plane)
    core = planes[:, :, 1 : depth + 1].reshape(cases_here, 3, groups, slab, plane)
    below = planes[:, :, 0:depth:slab][:, :, :, None]
    above = planes[:, :, slab + 1 : depth + 2 : slab][:, :, :, None]
    pieces = jnp.concatenate([below, core, above], axis=3)
    arrived = lax.all_to_all(pieces, "case", split_axis=2, concat_axis=0, tiled=True)
    local_field = arrived.reshape(arrived.shape[0], 3, slab + 2, plane)
    start = lax.axis_index("case") * slab
    shear_slab = flat_layout(lax.dynamic_slice_in_dim(shear_mod, start, slab, 2), slab)
    first_slab = flat_layout(lax.dynamic_slice_in_dim(lame_first, start, slab, 2), slab)
    weight_full = jnp.broadcast_to(
        lax.dynamic_slice_in_dim(weight, start, slab, 2), (rows, cols, slab)
    )
    weight_slab = flat_layout(weight_full, slab)
    stress = flat_stress(local_field, shear_slab, first_slab, weight_slab, width).astype(
        jnp.bfloat16
    )
    blocks = stress.reshape(stress.shape[0], 6, slab, rows, 1, width)
    peak_flat, spread_flat = histories(load_history, blocks)
    peak = jnp.transpose(peak_flat, (1, 2, 0))[:, 1 : cols + 1, :]
    spread = jnp.transpose(spread_flat, (1, 2, 0))[:, 1 : cols + 1, :]
    return (peak, spread)


def solution(mesh):
    in_specs = (P("case", None, "bx", "by", None), P("bx", "by", None), P(), P(None, "bx"), P())
    out_specs = (P("bx", "by", "case"), P("bx", "by", "case"))
    return jax.shard_map(shards, mesh=mesh, in_specs=in_specs, out_specs=out_specs, check_vma=False)
```

profile of v0, /device:TPU:6, one launch (start us, length us, event | category | flops | bytes accessed | tf_op | source)
XLA Modules:
  0.0 93.3 jit_solution(1109385592780561739)
XLA Ops:
  0.6 0.8 fusion.116
  1.4 3.5 %collective-permute-start.1 = (bf16[2,3,1,8,256]{4,3,2,1,0:T(8,128)(2,1)S(1)}, bf16[2,3,1,8,256]{4,3,2,1,0:T(8,128)(2,1)S(1)}, u32[]{:S(2)}, u32[]{:S(2)}) collective-permute-start(bf16[2,3,1,8,256]{4,3,2,1,0:T(8,128)(2,1)S(1)} %get-tuple-element.40), channel_id=1, source_target_pairs={{0,2},{2,4},{4,6},{6,8},{8,10},{10,12},{12,14},{1,3},{3,5},{5,7},{... | collective-permute-start | bytes 73736 | tf_op jit(solution)/shard_map/ppermute | solution.py:15
  4.9 4.5 %collective-permute-start.2 = (bf16[2,3,1,8,256]{4,3,2,1,0:T(8,128)(2,1)S(1)}, bf16[2,3,1,8,256]{4,3,2,1,0:T(8,128)(2,1)S(1)}, u32[]{:S(2)}, u32[]{:S(2)}) collective-permute-start(bf16[2,3,1,8,256]{4,3,2,1,0:T(8,128)(2,1)S(1)} %get-tuple-element.41), channel_id=1, source_target_pairs={{2,0},{4,2},{6,4},{8,6},{10,8},{12,10},{14,12},{3,1},{5,3},{7,5},{... | collective-permute-start | bytes 73736 | tf_op jit(solution)/shard_map/ppermute | solution.py:16
  9.3 1.1 %fusion.117 = (bf16[2,3,8,1,256]{4,3,2,1,0:T(2,128)(2,1)S(1)}, bf16[2,3,8,1,256]{4,3,2,1,0:T(2,128)(2,1)S(1)}) fusion(bf16[2,3,8,8,256]{4,3,2,1,0:T(8,128)(2,1)} %param.5), kind=kLoop, calls=%fused_computation.218 | loop fusion | bytes 98304 | tf_op jit(solution)/shard_map/slice | solution.py:12
  10.5 1.3 %collective-permute-start = (bf16[2,3,8,1,256]{4,3,2,1,0:T(2,128)(2,1)S(1)}, bf16[2,3,8,1,256]{4,3,2,1,0:T(2,128)(2,1)S(1)}, u32[]{:S(2)}, u32[]{:S(2)}) collective-permute-start(bf16[2,3,8,1,256]{4,3,2,1,0:T(2,128)(2,1)S(1)} %get-tuple-element.42), channel_id=1, source_target_pairs={{0,1},{2,3},{4,5},{6,7},{8,9},{10,11},{12,13},{14,15},{16,17},{18,... | collective-permute-start | bytes 73736 | tf_op jit(solution)/shard_map/ppermute | solution.py:15
  11.8 1.3 %collective-permute-start.3 = (bf16[2,3,8,1,256]{4,3,2,1,0:T(2,128)(2,1)S(1)}, bf16[2,3,8,1,256]{4,3,2,1,0:T(2,128)(2,1)S(1)}, u32[]{:S(2)}, u32[]{:S(2)}) collective-permute-start(bf16[2,3,8,1,256]{4,3,2,1,0:T(2,128)(2,1)S(1)} %get-tuple-element.43), channel_id=1, source_target_pairs={{1,0},{3,2},{5,4},{7,6},{9,8},{11,10},{13,12},{15,14},{17,16},{19,... | collective-permute-start | bytes 73736 | tf_op jit(solution)/shard_map/ppermute | solution.py:16
  13.1 0.8 slice_bitcast_fusion.28
  14.0 0.9 collective-permute-done.3
  14.9 1.3 %fusion.2 = bf16[2,3,10,10,256]{4,3,2,1,0:T(8,128)(2,1)S(1)} fusion(bf16[2,3,8,1,256]{4,3,2,1,0:T(2,128)(2,1)S(1)} %collective-permute-done.3, bf16[2,3,8,1,256]{4,3,2,1,0:T(2,128)(2,1)S(1)} %collective-permute-done, bf16[2,3,1,8,256]{4,3,2,1,0:T(8,128)(2,1)S(1)} %collective-permute-done.2, bf16[2,3,8,8,256]{4,3,2,1,0:T(8,128)(2,1)} %param.5, ...), kind=kLoop, calls=%fused_computation.7 | loop fusion | flops 2150400 | bytes 602112 | tf_op jit(solution)/shard_map/concatenate | solution.py:22
  16.8 5.2 %slice.396 = bf16[2,3,32,100]{2,0,3,1:T(2,128)(2,1)S(1)} slice(bf16[2,3,258,100]{2,0,3,1:T(2,128)(2,1)S(1)} %bitcast.396), slice={[0:2:1], [0:3:1], [9:258:8], [0:100:1]} | slice | bytes 76800 | tf_op jit(solution)/shard_map/slice | solution.py:130
  22.0 5.2 %slice.394 = bf16[2,3,32,100]{2,0,3,1:T(2,128)(2,1)S(1)} slice(bf16[2,3,258,100]{2,0,3,1:T(2,128)(2,1)S(1)} %bitcast.397), slice={[0:2:1], [0:3:1], [0:256:8], [0:100:1]} | slice | bytes 76800 | tf_op jit(solution)/shard_map/slice | solution.py:129
  27.3 0.5 slice.494
  28.1 0.6 copy.36
  28.8 0.5 pad_maximum_fusion
  29.3 1.4 %copy.39 = bf16[2,3,32,10,100]{4,0,3,1,2:T(2,128)(2,1)} copy(bf16[2,3,32,10,100]{4,3,2,1,0:T(8,128)(2,1)S(1)} %pad_maximum_fusion) | data formatting | bytes 768000 | tf_op jit(solution)/shard_map/concatenate | solution.py:131
  30.7 18.2 %all-to-all-start = ((bf16[2,3,32,10,100]{4,0,3,1,2:T(2,128)(2,1)}), bf16[2,3,32,10,100]{4,0,3,1,2:T(2,128)(2,1)S(1)}, u32[]{:S(2)}, u32[]{:S(2)}) async-start(bf16[2,3,32,10,100]{4,0,3,1,2:T(2,128)(2,1)} %copy.39), calls=%async_computation | async-start | bytes 983040 | tf_op jit(solution)/shard_map/all_to_all | solution.py:132
  49.2 0.7 fusion.118
  50.0 1.2 %select_select_fusion = (f32[8,8,256]{2,1,0:T(8,128)S(1)}, pred[8,8,256]{2,1,0:T(8,128)(4,1)S(1)}, pred[8,8,256]{2,1,0:T(8,128)(4,1)S(1)}) fusion(f32[]{:T(128)} %bitcast.27, f32[]{:T(128)} %bitcast.26, s32[8,8,256]{2,1,0:T(8,128)S(1)} %copy-done), kind=kLoop, calls=%fused_computation.151 | loop fusion | flops 65536 | bytes 163848 | tf_op jit(solution)/shard_map/jit(_where)/select_n | solution.py:70
  51.2 3.9 %fusion.74 = f32[8,8,8]{2,1,0:T(8,128)S(1)} fusion(f32[8,8,256]{2,1,0:T(8,128)S(1)} %get-tuple-element.34, s32[]{:T(128)S(6)} %select_n.62, pred[8,8,256]{2,1,0:T(8,128)(4,1)S(1)} %get-tuple-element.49, pred[8,8,256]{2,1,0:T(8,128)(4,1)S(1)} %get-tuple-element.48, pred[8,8,256]{2,1,0:T(8,128)(4,1)S(1)} %get-tuple-element.47, ...), kind=kLoop, calls=%fused_computation.159 | loop fusion | flops 3072 | bytes 7196 | tf_op jit(solution)/shard_map/jit(_where)/select_n | solution.py:70
  55.4 1.2 %select_select_fusion.1 = f32[8,8,256]{2,1,0:T(8,128)S(1)} fusion(pred[8,8,256]{2,1,0:T(8,128)(4,1)S(1)} %get-tuple-element.36, pred[8,8,256]{2,1,0:T(8,128)(4,1)S(1)} %get-tuple-element.35, f32[]{:T(128)} %bitcast.18, f32[]{:T(128)} %bitcast.17), kind=kLoop, calls=%fused_computation.153 | loop fusion | flops 32768 | bytes 98312 | tf_op jit(solution)/shard_map/jit(_where)/select_n | solution.py:71
  56.5 3.9 %fusion.79 = f32[8,8,8]{2,1,0:T(8,128)S(1)} fusion(f32[8,8,256]{2,1,0:T(8,128)S(1)} %select_select_fusion.1, s32[]{:T(128)S(6)} %select_n.62, pred[8,8,256]{2,1,0:T(8,128)(4,1)S(1)} %get-tuple-element.49, pred[8,8,256]{2,1,0:T(8,128)(4,1)S(1)} %get-tuple-element.48, pred[8,8,256]{2,1,0:T(8,128)(4,1)S(1)} %get-tuple-element.47, ...), kind=kLoop, calls=%fused_computation.165 | loop fusion | flops 3072 | bytes 7196 | tf_op jit(solution)/shard_map/jit(_where)/select_n | solution.py:71
  60.7 19.3 %all-to-all-done = bf16[2,3,32,10,100]{4,0,3,1,2:T(2,128)(2,1)S(1)} async-done(((bf16[2,3,32,10,100]{4,0,3,1,2:T(2,128)(2,1)}), bf16[2,3,32,10,100]{4,0,3,1,2:T(2,128)(2,1)S(1)}, u32[]{:S(2)}, u32[]{:S(2)}) %all-to-all-start) | async-done | bytes 384032 | tf_op jit(solution)/shard_map/all_to_all | solution.py:132
  80.3 0.5 copy.40
  82.9 0.5 copy.44
  83.4 0.8 reshape_reshape.3
  85.2 0.5 fusion.84
  88.0 0.9 fusion.113
  88.8 0.9 fusion.109
  89.7 0.9 fusion.105
  90.5 0.9 fusion.101
  91.6 0.7 copy.46
  92.6 0.7 copy.45
  (47 shorter events, 7.9 us)
Async XLA Ops:
  1.4 12.6 %collective-permute-start.1 = (bf16[2,3,1,8,256]{4,3,2,1,0:T(8,128)(2,1)S(1)}, bf16[2,3,1,8,256]{4,3,2,1,0:T(8,128)(2,1)S(1)}, u32[]{:S(2)}, u32[]{:S(2)}) collective-permute-start(bf16[2,3,1,8,256]{4,3,2,1,0:T(8,128)(2,1)S(1)} %get-tuple-element.40), channel_id=1, source_target_pairs={{0,2},{2,4},{4,6},{6,8},{8,10},{10,12},{12,14},{1,3},{3,5},{5,7},{... | collective-permute-start | bytes 73736 | tf_op jit(solution)/shard_map/ppermute | solution.py:15
  4.9 9.1 %collective-permute-start.2 = (bf16[2,3,1,8,256]{4,3,2,1,0:T(8,128)(2,1)S(1)}, bf16[2,3,1,8,256]{4,3,2,1,0:T(8,128)(2,1)S(1)}, u32[]{:S(2)}, u32[]{:S(2)}) collective-permute-start(bf16[2,3,1,8,256]{4,3,2,1,0:T(8,128)(2,1)S(1)} %get-tuple-element.41), channel_id=1, source_target_pairs={{2,0},{4,2},{6,4},{8,6},{10,8},{12,10},{14,12},{3,1},{5,3},{7,5},{... | collective-permute-start | bytes 73736 | tf_op jit(solution)/shard_map/ppermute | solution.py:16
  10.5 3.5 %collective-permute-start = (bf16[2,3,8,1,256]{4,3,2,1,0:T(2,128)(2,1)S(1)}, bf16[2,3,8,1,256]{4,3,2,1,0:T(2,128)(2,1)S(1)}, u32[]{:S(2)}, u32[]{:S(2)}) collective-permute-start(bf16[2,3,8,1,256]{4,3,2,1,0:T(2,128)(2,1)S(1)} %get-tuple-element.42), channel_id=1, source_target_pairs={{0,1},{2,3},{4,5},{6,7},{8,9},{10,11},{12,13},{14,15},{16,17},{18,... | collective-permute-start | bytes 73736 | tf_op jit(solution)/shard_map/ppermute | solution.py:15
  11.8 3.1 %collective-permute-start.3 = (bf16[2,3,8,1,256]{4,3,2,1,0:T(2,128)(2,1)S(1)}, bf16[2,3,8,1,256]{4,3,2,1,0:T(2,128)(2,1)S(1)}, u32[]{:S(2)}, u32[]{:S(2)}) collective-permute-start(bf16[2,3,8,1,256]{4,3,2,1,0:T(2,128)(2,1)S(1)} %get-tuple-element.43), channel_id=1, source_target_pairs={{1,0},{3,2},{5,4},{7,6},{9,8},{11,10},{13,12},{15,14},{17,16},{19,... | collective-permute-start | bytes 73736 | tf_op jit(solution)/shard_map/ppermute | solution.py:16
  28.7 20.4 %copy-start.2 = (f32[2,8]{1,0:T(2,128)S(1)}, f32[2,8]{1,0:T(2,128)}, u32[]{:S(2)}) copy-start(f32[2,8]{1,0:T(2,128)} %param.7) | copy-start | bytes 196
  28.7 21.2 %copy-start = (s32[8,8,256]{2,1,0:T(8,128)S(1)}, s32[8,8,256]{2,1,0:T(8,128)}, u32[]{:S(2)}) copy-start(s32[8,8,256]{2,1,0:T(8,128)} %param.6) | copy-start | bytes 196612
  30.7 49.3 %all-to-all-start = ((bf16[2,3,32,10,100]{4,0,3,1,2:T(2,128)(2,1)}), bf16[2,3,32,10,100]{4,0,3,1,2:T(2,128)(2,1)S(1)}, u32[]{:S(2)}, u32[]{:S(2)}) async-start(bf16[2,3,32,10,100]{4,0,3,1,2:T(2,128)(2,1)} %copy.39), calls=%async_computation | async-start | bytes 983040 | tf_op jit(solution)/shard_map/all_to_all | solution.py:132
  82.6 1.7 %copy-start.1 = (bf16[1024,64]{0,1:T(8,128)(2,1)S(1)}, bf16[1024,64]{0,1:T(8,128)(2,1)}, u32[]{:S(2)}) copy-start(bf16[1024,64]{0,1:T(8,128)(2,1)} %param.9) | copy-start | bytes 393220
where the time goes:
time: 93.8 us; the launch traced here: 93.3 us
  starting transfers between devices  28.7 us (31%)
  local copies, waits for them, and re-layouts  21.8 us (23%)
  waiting for transfers between devices  20.2 us (22%)
  other arithmetic  17.9 us (19%)
  matrix products  3.67 us (4%)
  between operations  0.95 us (1%)
    all_to_all x1, waiting for transfers between devices, shards(): lax.all_to_all(pieces, 'case', split_axis=2, concat_axis=0, tiled=True)  19.3 us
    all_to_all x1, starting transfers between devices, shards(): lax.all_to_all(pieces, 'case', split_axis=2, concat_axis=0, tiled=True)  18.2 us
    ppermute x2, starting transfers between devices, with_halo(): lax.ppermute(leading, axis, [(b, a) for a, b in up])  5.76 us
    slice x1, local copies, waits for them, and re-layouts, shards(): below = planes[:, :, 0:depth:slab][:, :, :, None]  5.22 us
    slice x1, local copies, waits for them, and re-layouts, shards(): above = planes[:, :, slab + 1:depth + 2:slab][:, :, :, None]  5.21 us
    select_n x2, other arithmetic, material_moduli(): shear_mod = jnp.where(picked, lame[0, material], shear_mod)  5.14 us
    select_n x2, other arithmetic, material_moduli(): lame_first = jnp.where(picked, lame[1, material], lame_first)  5.11 us
    ppermute x2, starting transfers between devices, with_halo(): lax.ppermute(last, axis, up)  4.76 us
  transfers between devices with their start and end apart: 5, of which 2 were waited for; matrix products, arithmetic and copies ran while one was open for 15% of the time, Pallas kernels for 0%

commit v1 on v0

v1 whole, which is shorter than its diff:
```python
import functools
import math

import jax
import jax.numpy as jnp
from jax import lax
from jax.experimental import pallas as pl
from jax.experimental.pallas import tpu as pltpu
from jax.sharding import PartitionSpec as P

MESH = pl.DeviceIdType.MESH
F32 = jnp.float32
BF16 = jnp.bfloat16


def z_offsets(chips):
    half = chips // 2
    offsets = [half]
    for distance in range(half - 1, 0, -1):
        offsets += [distance, -distance]
    return offsets + [0]


def slot_of(chips, offset, flip):
    return 2 * z_offsets(chips).index(offset) + 1 - flip


def kernel(
    chips, cuts, disp_ref, mat_ref, lame_ref, bounds_ref, hist_ref, peak_ref, range_ref,
    turned, edge, send, own, low, high, side, moduli, weights, factors, cells, rhs, rhs_shear,
    sent, got, moved, moved_sent, local,
):
    case = lax.axis_index("case")
    bx = lax.axis_index("bx")
    by = lax.axis_index("by")
    bricks = lax.axis_size("bx")
    chip_z = case // 2
    half = lax.rem(case, 2)
    slots = 2 * chips

    def peer(offset, flip):
        return lax.rem(chip_z + offset + chips, chips) * 2 + lax.rem(half + flip, 2)

    offsets = [(dz, flip) for dz in z_offsets(chips) for flip in (1, 0)][:-1]
    x_next = {"bx": lax.rem(bx + 1, bricks)}
    x_prev = {"bx": lax.rem(bx + bricks - 1, bricks)}
    partner = {"by": 1 - by}

    barrier = pltpu.get_barrier_semaphore()
    for dz, flip in offsets:
        pl.semaphore_signal(barrier, inc=1, device_id={"case": peer(dz, flip)}, device_id_type=MESH)
    for target in (x_next, x_prev, partner):
        pl.semaphore_signal(barrier, inc=1, device_id=target, device_id_type=MESH)

    zero_rows = jnp.zeros((8, 128), F32)
    for a in range(3):
        first = disp_ref[0, a].astype(F32).reshape(64, 256)
        second = disp_ref[1, a].astype(F32).reshape(64, 256)
        flat = jnp.concatenate([first, second], axis=0)
        turned[a, 0:8] = zero_rows
        turned[a, 264:272] = zero_rows
        turned[a, 8:264] = flat.T
        send[:, a] = turned[a, 8:264].reshape(slots, 8, 128).astype(BF16)
        edge[pl.ds(2 * a, slots, stride=8), :] = turned[a, pl.ds(7, slots, stride=8), :]
        edge[pl.ds(2 * a + 1, slots, stride=8), :] = turned[a, pl.ds(16, slots, stride=8), :]
    edge[pl.ds(6, slots, stride=8), :] = jnp.zeros((slots, 128), F32)
    edge[pl.ds(7, slots, stride=8), :] = jnp.zeros((slots, 128), F32)
    send[:, 3] = edge[...].reshape(slots, 8, 128).astype(BF16)

    mine = pltpu.make_async_copy(send.at[case], own.at[slots - 1], local)
    mine.start()
    pl.semaphore_wait(barrier, len(offsets) + 3)
    for dz, flip in offsets:
        target = peer(dz, flip)
        back = dz if dz == chips // 2 else -dz
        slot = slot_of(chips, back, flip)
        group = [g for g in range(len(cuts) - 1) if cuts[g] <= slot < cuts[g + 1]][0]
        pltpu.make_async_remote_copy(
            src_ref=send.at[target],
            dst_ref=own.at[slot],
            send_sem=sent,
            recv_sem=got.at[group],
            device_id={"case": target},
            device_id_type=MESH,
        ).start()

    flat = mat_ref[...].astype(F32).reshape(64, 256)
    moduli[...] = jnp.concatenate([flat, flat], axis=0).T
    phase = moduli[pl.ds(pl.multiple_of(8 * case, 8), 8), :].astype(jnp.int32)
    lane = lax.broadcasted_iota(jnp.int32, (8, 128), 1)
    level = lax.broadcasted_iota(jnp.int32, (8, 128), 0) + 8 * case
    column = (lane // 8) % 8
    shear_mod = jnp.zeros((8, 128), F32)
    lame_first = jnp.zeros((8, 128), F32)
    bottom = jnp.zeros((8, 128), jnp.int32)
    top = jnp.zeros((8, 128), jnp.int32)
    for m in range(8):
        shear_mod = jnp.where(phase == m, lame_ref[0, m], shear_mod)
        lame_first = jnp.where(phase == m, lame_ref[1, m], lame_first)
        bottom = jnp.where(column == m, bounds_ref[0, m], bottom)
        top = jnp.where(column == m, bounds_ref[1, m], top)
    weight = ((bottom <= level) & (level < top)).astype(F32)
    shear_mod = shear_mod * weight
    lame_first = lame_first * weight

    r = lax.broadcasted_iota(jnp.int32, (128, 128), 0)
    c = lax.broadcasted_iota(jnp.int32, (128, 128), 1)
    cx = (c // 8) % 8
    cy = c % 8

    def picked(plus, minus):
        return jnp.where(plus, 0.5, jnp.where(minus, -0.5, 0.0)).astype(BF16)

    never = r < 0
    has_low = jnp.full((128, 128), bx, jnp.int32) > 0
    has_high = jnp.full((128, 128), bx, jnp.int32) < bricks - 1
    upper = jnp.full((128, 128), by, jnp.int32) > 0
    weights[0:128, 0:128] = picked((r == c + 8) & (cx < 7), (r == c - 8) & (cx > 0))
    weights[0:128, 128:256] = picked((r == c + 1) & (cy < 7), (r == c - 1) & (cy > 0))
    weights[128:256, 0:128] = picked(never, (r == c + 56) & (cx == 0) & has_low)
    weights[256:384, 0:128] = picked((r == c - 56) & (cx == 7) & has_high, never)
    weights[128:256, 128:256] = jnp.zeros((128, 128), BF16)
    weights[256:384, 128:256] = jnp.zeros((128, 128), BF16)
    weights[384:512, 0:128] = jnp.zeros((128, 128), BF16)
    weights[384:512, 128:256] = picked(
        (r == c - 7) & (cy == 7) & jnp.logical_not(upper), (r == c + 7) & (cy == 0) & upper
    )

    r = lax.broadcasted_iota(jnp.int32, (64, 128), 0)
    c = lax.broadcasted_iota(jnp.int32, (64, 128), 1)
    slot = c % slots
    pair = (c // slots) % 2
    zi = slot // 2
    far = chips // 2 - (zi + 1) // 2
    dz = jnp.where(zi % 2 == 1, far, jnp.where(zi == 0, far, -far))
    source = ((chip_z + dz + chips) % chips) * 2 + (half + 1 - slot % 2) % 2
    order = (r == 2 * source + pair).astype(F32).astype(BF16)
    steps = hist_ref.shape[1]
    for begin in range(0, steps, 256):
        block = hist_ref[:, begin : begin + 256].astype(F32).T.astype(BF16)
        factors[begin : begin + 256, :] = jnp.dot(
            block, order, preferred_element_type=F32
        ).astype(BF16)

    mine.wait()
    groups = len(cuts) - 1
    forwards = []
    for g in range(groups):
        lo, hi = cuts[g], cuts[g + 1]
        arrived = own.at[pl.ds(lo, min(hi, slots - 1) - lo)]
        pltpu.make_async_remote_copy(
            src_ref=arrived, dst_ref=arrived, send_sem=sent, recv_sem=got.at[g],
            device_id=partner, device_id_type=MESH,
        ).wait_recv()
        for k, (target, place) in enumerate(((x_next, low), (x_prev, high), (partner, side))):
            move = pltpu.make_async_remote_copy(
                src_ref=own.at[pl.ds(lo, hi - lo), pl.ds(0, 3)],
                dst_ref=place.at[pl.ds(lo, hi - lo)],
                send_sem=moved_sent.at[k, g],
                recv_sem=moved.at[k, g],
                device_id=target,
                device_id_type=MESH,
            )
            move.start()
            forwards.append(move)

    row = lax.broadcasted_iota(jnp.int32, (8, 8, 128), 1)
    for g in range(groups):
        for k in range(3):
            forwards[3 * g + k].wait_recv()
        for s0 in range(cuts[g], cuts[g + 1], 8):
            here = [ref[s0 : s0 + 8, 0:3].astype(F32) for ref in (own, low, high, side)]
            flat = jnp.concatenate(
                [part.reshape(192, 128).astype(BF16) for part in here], axis=1
            )
            planar = jnp.dot(flat, weights[...], preferred_element_type=F32)
            along_x = planar[:, 0:128].reshape(8, 3, 8, 128)
            along_y = planar[:, 128:256].reshape(8, 3, 8, 128)
            halo = own[s0 : s0 + 8, 3].astype(F32)
            along_z = []
            for a in range(3):
                field = here[0][:, a]
                up = jnp.where(row == 7, halo[:, 2 * a + 1 : 2 * a + 2], pltpu.roll(field, 7, 1))
                down = jnp.where(row == 0, halo[:, 2 * a : 2 * a + 1], pltpu.roll(field, 1, 1))
                along_z.append(0.5 * (up - down))
            g_xx, g_yy, g_zz = along_x[:, 0], along_y[:, 1], along_z[2]
            spread = lame_first * (g_xx + g_yy + g_zz)
            double = 2.0 * shear_mod
            rounded = [
                value.astype(BF16).astype(F32)
                for value in (
                    spread + double * g_xx,
                    spread + double * g_yy,
                    spread + double * g_zz,
                    shear_mod * (along_y[:, 0] + along_x[:, 1]),
                    shear_mod * (along_z[1] + along_y[:, 2]),
                    shear_mod * (along_x[:, 2] + along_z[0]),
                )
            ]
            s_x, s_y, s_z = rounded[:3]
            values = [
                0.5 * (s_x - s_y),
                (s_x + s_y - 2.0 * s_z) * (0.5 / math.sqrt(3.0)),
                s_x + s_y + s_z,
            ] + rounded[3:]
            for k in range(6):
                for i in range(8):
                    cells[k, pl.ds(s0 + i, 8, stride=slots), :] = values[k][i]

    lane = lax.broadcasted_iota(jnp.int32, (slots, 128), 1)
    for k in range(6):
        for p in range(4):
            even = cells[k, 2 * p * slots : (2 * p + 1) * slots]
            odd = cells[k, (2 * p + 1) * slots : (2 * p + 2) * slots]
            first = jnp.where(lane < 64, even, pltpu.roll(odd, 64, 1))
            second = jnp.where(lane < 64, pltpu.roll(even, 64, 1), odd)
            both = jnp.concatenate([first, second], axis=0)
            coarse = both.astype(BF16)
            if k < 3:
                fine = (both - coarse.astype(F32)).astype(BF16)
                rhs[k, 0:64, 128 * p : 128 * (p + 1)] = coarse
                rhs[k, 64:128, 128 * p : 128 * (p + 1)] = fine
            else:
                rhs_shear[k - 3, :, 128 * p : 128 * (p + 1)] = coarse

    block = 256
    results = []
    for n in range(2):
        columns = slice(256 * n, 256 * (n + 1))

        def body(i, carry):
            most, upper_h, lower_h = carry
            full = factors[pl.ds(pl.multiple_of(i * block, block), block), :]
            total = None
            for k in (0, 1):
                part = jnp.dot(full, rhs[k, :, columns], preferred_element_type=F32)
                total = part * part if total is None else total + part * part
            for k in range(3):
                part = jnp.dot(full[:, 0:64], rhs_shear[k, :, columns], preferred_element_type=F32)
                total = total + part * part
            mean = jnp.dot(full, rhs[2, :, columns], preferred_element_type=F32)
            total = total.reshape(block // 8, 8, 256)
            mean = mean.reshape(block // 8, 8, 256)
            return (
                jnp.maximum(most, jnp.max(total, axis=0)),
                jnp.maximum(upper_h, jnp.max(mean, axis=0)),
                jnp.minimum(lower_h, jnp.min(mean, axis=0)),
            )

        start = (
            jnp.zeros((8, 256), F32),
            jnp.full((8, 256), -jnp.inf, F32),
            jnp.full((8, 256), jnp.inf, F32),
        )
        most, upper_h, lower_h = lax.fori_loop(0, steps // block, body, start)
        most = jnp.max(most, axis=0, keepdims=True)
        upper_h = jnp.max(upper_h, axis=0, keepdims=True)
        lower_h = jnp.min(lower_h, axis=0, keepdims=True)
        results.append((jnp.sqrt(3.0 * most), (upper_h - lower_h) * (1.0 / 3.0)))

    for which, out_ref in ((0, peak_ref), (1, range_ref)):
        rows = []
        for n in range(2):
            for p in range(2):
                pair_row = results[n][which][:, 128 * p : 128 * (p + 1)]
                rows += [pair_row, pltpu.roll(pair_row, 64, 1)]
        out_ref[...] = jnp.concatenate(rows, axis=0).T[0:64].reshape(8, 8, 8)

    whole = send.at[pl.ds(0, slots - 1)]
    pltpu.make_async_remote_copy(
        src_ref=whole, dst_ref=whole, send_sem=sent, recv_sem=got.at[0],
        device_id=partner, device_id_type=MESH,
    ).wait_send()
    for move in forwards:
        move.wait_send()


def shards(displacements, material_ids, lame, slab_bounds, load_history):
    chips = lax.axis_size("case") // 2
    slots = 2 * chips
    cuts = (0, 8, 16, 24, 32)
    groups = len(cuts) - 1
    vmem = pl.BlockSpec(memory_space=pltpu.VMEM)
    smem = pl.BlockSpec(memory_space=pltpu.SMEM)
    steps = load_history.shape[0]
    shape = jax.ShapeDtypeStruct((8, 8, 8), F32)
    return pl.pallas_call(
        functools.partial(kernel, chips, cuts),
        out_shape=(shape, shape),
        in_specs=[vmem, vmem, smem, smem, vmem],
        out_specs=(vmem, vmem),
        scratch_shapes=[
            pltpu.VMEM((3, 272, 128), F32),
            pltpu.VMEM((8 * slots, 128), F32),
            pltpu.VMEM((slots, 4, 8, 128), BF16),
            pltpu.VMEM((slots, 4, 8, 128), BF16),
            pltpu.VMEM((slots, 3, 8, 128), BF16),
            pltpu.VMEM((slots, 3, 8, 128), BF16),
            pltpu.VMEM((slots, 3, 8, 128), BF16),
            pltpu.VMEM((256, 128), F32),
            pltpu.VMEM((512, 256), BF16),
            pltpu.VMEM((steps, 128), BF16),
            pltpu.VMEM((6, 8 * slots, 128), F32),
            pltpu.VMEM((3, 128, 512), BF16),
            pltpu.VMEM((3, 64, 512), BF16),
            pltpu.SemaphoreType.DMA,
            pltpu.SemaphoreType.DMA((groups,)),
            pltpu.SemaphoreType.DMA((3, groups)),
            pltpu.SemaphoreType.DMA((3, groups)),
            pltpu.SemaphoreType.DMA,
        ],
        compiler_params=pltpu.CompilerParams(collective_id=0, has_side_effects=True),
    )(displacements, material_ids, lame, slab_bounds, load_history.T)


def solution(mesh):
    in_specs = (P("case", None, "bx", "by", None), P("bx", "by", None), P(), P(None, "bx"), P())
    out_specs = (P("bx", "by", "case"), P("bx", "by", "case"))
    return jax.shard_map(shards, mesh=mesh, in_specs=in_specs, out_specs=out_specs, check_vma=False)
```

time: 93.8 us -> 44.1 us (0.47)
  the two profiles are of different devices: /device:TPU:6 before, /device:TPU:4 now
where the time goes in v1:
time: 44.1 us; the launch traced here: 43.9 us
  Pallas kernels  41.2 us (93%)
  local copies, waits for them, and re-layouts  2 us (5%)
  between operations  0.65 us (1%)
    pallas_call x1, Pallas kernels, shards(): pl.pallas_call(functools.partial(kernel, chips, cuts), out_shape=(shape,...  41.2 us
    unnamed x4, local copies, waits for them, and re-layouts  2 us

profile of v1, /device:TPU:4, one launch (start us, length us, event | category | flops | bytes accessed | tf_op | source)
XLA Modules:
  0.0 43.9 jit_solution(7450664042898035)
XLA Ops:
  0.6 41.2 %shard_map.68 = (f32[8,8,8]{2,1,0:T(8,128)}, f32[8,8,8]{2,1,0:T(8,128)}) custom-call(bf16[2,3,8,8,256]{4,3,2,1,0:T(8,128)(2,1)} %disp_ref.1, s32[8,8,256]{2,1,0:T(8,128)} %mat_ref.1, f32[2,8]{1,0:T(2,128)} %lame_ref.1, s32[2,8]{1,0:T(2,128)} %bounds_ref.1, bf16[64,1024]{1,0:T(8,128)(2,1)} %bitcast.1), custom_call_target="tpu_custom_call" | custom-call | tf_op jit(solution)/shard_map/pallas_call | solution.py:287
  41.8 0.0 copy-start
  41.9 1.4 %copy.9 = f32[8,8,8]{2,1,0:T(8,128)} copy(f32[8,8,8]{2,1,0:T(8,128)} %get-tuple-element.4) | data formatting | bytes 4096
  43.2 0.0 copy-done
  43.2 0.6 %copy.10 = f32[8,8,8]{2,1,0:T(8,128)} copy(f32[8,8,8]{2,1,0:T(8,128)S(1)} %copy-done) | data formatting | bytes 4096
Async XLA Ops:
  41.8 1.4 %copy-start = (f32[8,8,8]{2,1,0:T(8,128)S(1)}, f32[8,8,8]{2,1,0:T(8,128)}, u32[]{:S(2)}) copy-start(f32[8,8,8]{2,1,0:T(8,128)} %get-tuple-element.5) | copy-start | bytes 6148

commit v2 on v1

v2 whole, which is shorter than its diff:
```python
import functools
import math

import jax
import jax.numpy as jnp
from jax import lax
from jax.experimental import pallas as pl
from jax.experimental.pallas import tpu as pltpu
from jax.sharding import PartitionSpec as P

MESH = pl.DeviceIdType.MESH
F32 = jnp.float32
BF16 = jnp.bfloat16
GROUP = 8


def kernel(
    order, disp_any, mat_any, lame_any, bounds_any, hist_any, most_ref, spread_ref,
    disp_ref, mat_ref, lame_ref, bounds_ref, hist_ref, loaded,
    turned, send, own, faces, halos, rows_ref, halo_rows, moduli, weights, factors, cells, rhs, rhs_shear,
    sent, got, face_sent, face_got,
):
    case = lax.axis_index("case")
    bx = lax.axis_index("bx")
    by = lax.axis_index("by")
    bricks = lax.axis_size("bx")
    slots = lax.axis_size("case")
    x_next = {"bx": lax.rem(bx + 1, bricks)}
    x_prev = {"bx": lax.rem(bx + bricks - 1, bricks)}
    partner = {"by": 1 - by}
    above = {"case": lax.rem(case + 1, slots)}
    below = {"case": lax.rem(case + slots - 1, slots)}

    barrier = pltpu.get_barrier_semaphore()
    for target in range(slots):
        @pl.when(target != case)
        def _():
            pl.semaphore_signal(barrier, inc=1, device_id={"case": target}, device_id_type=MESH)
    for target in (x_next, x_prev, partner):
        pl.semaphore_signal(barrier, inc=1, device_id=target, device_id_type=MESH)

    loads = [
        pltpu.make_async_copy(src, dst, loaded.at[i])
        for i, (src, dst) in enumerate(
            (
                (disp_any, disp_ref),
                (hist_any, hist_ref),
                (mat_any, mat_ref),
                (lame_any, lame_ref),
                (bounds_any, bounds_ref),
            )
        )
    ]
    for load in loads:
        load.start()

    loads[0].wait()
    for a in range(3):
        first = disp_ref[0, a].astype(F32).reshape(64, 256)
        second = disp_ref[1, a].astype(F32).reshape(64, 256)
        turned[...] = jnp.concatenate([first, second], axis=0).T
        send[:, a] = turned[...].reshape(slots, 8, 128).astype(BF16)

    pl.semaphore_wait(barrier, slots + 2)
    mine = pltpu.make_async_copy(send.at[case], own.at[case], got.at[case // GROUP])
    mine.start()
    for target in range(slots):
        @pl.when(target != case)
        def _():
            pltpu.make_async_remote_copy(
                src_ref=send.at[target],
                dst_ref=own.at[case],
                send_sem=sent,
                recv_sem=got.at[case // GROUP],
                device_id={"case": target},
                device_id_type=MESH,
            ).start()

    loads[1].wait()
    r = lax.broadcasted_iota(jnp.int32, (64, 128), 0)
    c = lax.broadcasted_iota(jnp.int32, (64, 128), 1)
    permute = (r == 2 * (c % slots) + (c // slots) % 2).astype(F32).astype(BF16)
    steps = hist_ref.shape[1]
    for begin in range(0, steps, 256):
        block = hist_ref[:, begin : begin + 256].astype(F32).T.astype(BF16)
        factors[begin : begin + 256, :] = jnp.dot(
            block, permute, preferred_element_type=F32
        ).astype(BF16)

    for load in loads[2:]:
        load.wait()
    flat = mat_ref[...].astype(F32).reshape(64, 256)
    moduli[...] = jnp.concatenate([flat, flat], axis=0).T
    phase = moduli[pl.ds(pl.multiple_of(8 * case, 8), 8), :].astype(jnp.int32)
    lane = lax.broadcasted_iota(jnp.int32, (8, 128), 1)
    row = lax.broadcasted_iota(jnp.int32, (8, 128), 0)
    level = row + 8 * case
    column = (lane // 8) % 8
    shear_mod = jnp.zeros((8, 128), F32)
    lame_first = jnp.zeros((8, 128), F32)
    bottom = jnp.zeros((8, 128), jnp.int32)
    top = jnp.zeros((8, 128), jnp.int32)
    for m in range(8):
        shear_mod = jnp.where(phase == m, lame_ref[0, m], shear_mod)
        lame_first = jnp.where(phase == m, lame_ref[1, m], lame_first)
        bottom = jnp.where(column == m, bounds_ref[0, m], bottom)
        top = jnp.where(column == m, bounds_ref[1, m], top)
    weight = ((bottom <= level) & (level < top)).astype(F32)
    shear_mod = shear_mod * weight
    lame_first = lame_first * weight
    double = 2.0 * shear_mod

    r = lax.broadcasted_iota(jnp.int32, (128, 128), 0)
    c = lax.broadcasted_iota(jnp.int32, (128, 128), 1)
    cx = (c // 8) % 8
    cy = c % 8
    same = r // 64 == c // 64

    def picked(plus, minus):
        return jnp.where(plus, 0.5, jnp.where(minus, -0.5, 0.0)).astype(BF16)

    never = r < 0
    has_low = jnp.full((128, 128), bx, jnp.int32) > 0
    has_high = jnp.full((128, 128), bx, jnp.int32) < bricks - 1
    upper = jnp.full((128, 128), by, jnp.int32) > 0
    lower = jnp.full((128, 128), by, jnp.int32) < 1
    none = jnp.zeros((128, 128), BF16)
    weights[0:128, 0:128] = picked((r == c + 8) & (cx < 7), (r == c - 8) & (cx > 0))
    weights[0:128, 128:256] = picked((r == c + 1) & (cy < 7), (r == c - 1) & (cy > 0))
    weights[128:256, 0:128] = picked(never, same & (r % 8 == cy) & (cx == 0) & has_low)
    weights[256:384, 0:128] = picked(same & (r % 8 == cy) & (cx == 7) & has_high, never)
    weights[128:256, 128:256] = none
    weights[256:384, 128:256] = none
    weights[384:512, 0:128] = none
    alike = same & ((r // 8) % 8 == cx)
    weights[384:512, 128:256] = picked(alike & (cy == 7) & lower, alike & (cy == 0) & upper)

    in_upper = jnp.full((GROUP, 128), by, jnp.int32) > 0
    moves = {}

    @pl.when(case == 0)
    def _():
        halos[:, 3] = jnp.zeros(halos.shape[:1] + halos.shape[2:], BF16)

    @pl.when(case == slots - 1)
    def _():
        halos[:, 4] = jnp.zeros(halos.shape[:1] + halos.shape[2:], BF16)

    for g in order:
        s0 = GROUP * g
        arrived = own.at[pl.ds(s0, GROUP)]
        pltpu.make_async_remote_copy(
            src_ref=arrived, dst_ref=arrived, send_sem=sent, recv_sem=got.at[g],
            device_id=partner, device_id_type=MESH,
        ).wait_recv()
        rows_ref[g] = own[s0 : s0 + GROUP].astype(F32).reshape(24 * GROUP, 128)
        packed = [[], [], [], [], []]
        for a in range(3):
            to_next = to_prev = to_side = jnp.zeros((GROUP, 128), F32)
            for z in range(8):
                value = rows_ref[g, pl.ds(8 * a + z, GROUP, stride=24), :]
                to_next = jnp.where(column == z, pltpu.roll(value, (8 * z - 56) % 128, 1), to_next)
                to_prev = jnp.where(column == z, pltpu.roll(value, 8 * z, 1), to_prev)
                turn = jnp.where(in_upper, pltpu.roll(value, z, 1), pltpu.roll(value, (z - 7) % 128, 1))
                to_side = jnp.where(lane % 8 == z, turn, to_side)
                if z == 0:
                    packed[4].append(value)
                if z == 7:
                    packed[3].append(value)
            packed[0].append(to_next)
            packed[1].append(to_prev)
            packed[2].append(to_side)
        for k, target in enumerate((x_next, x_prev, partner, above, below)):
            for a in range(3):
                faces[g, k, a] = packed[k][a].astype(BF16)
            move = pltpu.make_async_remote_copy(
                src_ref=faces.at[g, k],
                dst_ref=halos.at[g, k],
                send_sem=face_sent.at[g, k],
                recv_sem=face_got.at[g, k],
                device_id=target,
                device_id_type=MESH,
            )
            moves[g, k] = move
            if k < 3:
                move.start()
            elif k == 3:
                pl.when(case < slots - 1)(move.start)
            else:
                pl.when(case > 0)(move.start)

    in_column = column == row
    in_row = lane % 8 == row
    for g in order:
        s0 = GROUP * g
        for k in range(5):
            if k < 3:
                moves[g, k].wait_recv()
            elif k == 3:
                pl.when(case > 0)(moves[g, k].wait_recv)
            else:
                pl.when(case < slots - 1)(moves[g, k].wait_recv)
            halo_rows[g, k] = halos[g, k].astype(F32).reshape(3 * GROUP, 128)

        def halo(k, i, a):
            at = GROUP * a + i
            return jnp.broadcast_to(halo_rows[g, k, at : at + 1, :], (8, 128))

        parts = [rows_ref[g]]
        for k, mask in ((0, in_column), (1, in_column), (2, in_row)):
            parts.append(
                jnp.concatenate(
                    [
                        jnp.where(mask, halo(k, i, a), 0.0)
                        for i in range(GROUP)
                        for a in range(3)
                    ],
                    axis=0,
                )
            )
        flat = jnp.concatenate([part.astype(BF16) for part in parts], axis=1)
        planar = jnp.dot(flat, weights[...], preferred_element_type=F32)
        for i in range(GROUP):
            grads = []
            for a in range(3):
                at = 24 * i + 8 * a
                field = rows_ref[g, at : at + 8]
                down = jnp.where(
                    row == 0,
                    halo(3, i, a),
                    pltpu.roll(field, 1, 0),
                )
                up = jnp.where(
                    row == 7,
                    halo(4, i, a),
                    pltpu.roll(field, 7, 0),
                )
                grads.append(
                    (planar[at : at + 8, 0:128], planar[at : at + 8, 128:256], 0.5 * (up - down))
                )
            g_xx, g_yy, g_zz = grads[0][0], grads[1][1], grads[2][2]
            spread = lame_first * (g_xx + g_yy + g_zz)
            s_x, s_y, s_z, s_xy, s_yz, s_zx = [
                value.astype(BF16).astype(F32)
                for value in (
                    spread + double * g_xx,
                    spread + double * g_yy,
                    spread + double * g_zz,
                    shear_mod * (grads[0][1] + grads[1][0]),
                    shear_mod * (grads[1][2] + grads[2][1]),
                    shear_mod * (grads[2][0] + grads[0][2]),
                )
            ]
            values = (
                0.5 * (s_x - s_y),
                (s_x + s_y - 2.0 * s_z) * (0.5 / math.sqrt(3.0)),
                s_x + s_y + s_z,
                s_xy,
                s_yz,
                s_zx,
            )
            for k in range(6):
                cells[k, pl.ds(s0 + i, 8, stride=slots), :] = values[k]

    left = lax.broadcasted_iota(jnp.int32, (slots, 128), 1) < 64
    for k in range(6):
        for p in range(4):
            even = cells[k, 2 * p * slots : (2 * p + 1) * slots]
            odd = cells[k, (2 * p + 1) * slots : (2 * p + 2) * slots]
            first = jnp.where(left, even, pltpu.roll(odd, 64, 1))
            second = jnp.where(left, pltpu.roll(even, 64, 1), odd)
            both = jnp.concatenate([first, second], axis=0)
            coarse = both.astype(BF16)
            if k < 3:
                fine = (both - coarse.astype(F32)).astype(BF16)
                rhs[k, 0:64, 128 * p : 128 * (p + 1)] = coarse
                rhs[k, 64:128, 128 * p : 128 * (p + 1)] = fine
            else:
                rhs_shear[k - 3, :, 128 * p : 128 * (p + 1)] = coarse

    block = 256
    results = []
    for n in range(2):
        columns = slice(256 * n, 256 * (n + 1))

        def body(i, carry):
            most, upper_h, lower_h = carry
            full = factors[pl.ds(pl.multiple_of(i * block, block), block), :]
            total = None
            for k in (0, 1):
                part = jnp.dot(full, rhs[k, :, columns], preferred_element_type=F32)
                total = part * part if total is None else total + part * part
            for k in range(3):
                part = jnp.dot(full[:, 0:64], rhs_shear[k, :, columns], preferred_element_type=F32)
                total = total + part * part
            mean = jnp.dot(full, rhs[2, :, columns], preferred_element_type=F32)
            total = total.reshape(block // 8, 8, 256)
            mean = mean.reshape(block // 8, 8, 256)
            return (
                jnp.maximum(most, jnp.max(total, axis=0)),
                jnp.maximum(upper_h, jnp.max(mean, axis=0)),
                jnp.minimum(lower_h, jnp.min(mean, axis=0)),
            )

        start = (
            jnp.zeros((8, 256), F32),
            jnp.full((8, 256), -jnp.inf, F32),
            jnp.full((8, 256), jnp.inf, F32),
        )
        most, upper_h, lower_h = lax.fori_loop(0, steps // block, body, start)
        most = jnp.max(most, axis=0, keepdims=True)
        upper_h = jnp.max(upper_h, axis=0, keepdims=True)
        lower_h = jnp.min(lower_h, axis=0, keepdims=True)
        results.append((most, upper_h - lower_h))

    for which, out_ref in ((0, most_ref), (1, spread_ref)):
        rows = []
        for n in range(2):
            for p in range(2):
                pair_row = results[n][which][:, 128 * p : 128 * (p + 1)]
                rows += [pair_row, pltpu.roll(pair_row, 64, 1)]
        out_ref[...] = jnp.concatenate(rows, axis=0).T[0:64].reshape(8, 8, 8)

    whole = send.at[pl.ds(0, slots - 1)]
    pltpu.make_async_remote_copy(
        src_ref=whole, dst_ref=whole, send_sem=sent, recv_sem=got.at[0],
        device_id=partner, device_id_type=MESH,
    ).wait_send()
    for (_, k), move in moves.items():
        if k < 3:
            move.wait_send()
        elif k == 3:
            pl.when(case < slots - 1)(move.wait_send)
        else:
            pl.when(case > 0)(move.wait_send)


def shards(displacements, material_ids, lame, slab_bounds, load_history):
    slots = lax.axis_size("case")
    groups = slots // GROUP
    steps = load_history.shape[0]
    anywhere = pl.BlockSpec(memory_space=pl.ANY)
    vmem = pl.BlockSpec(memory_space=pltpu.VMEM)
    shape = jax.ShapeDtypeStruct((8, 8, 8), F32)
    factors = load_history.T
    most, spread = pl.pallas_call(
        functools.partial(kernel, (0, 1, 3, 2)),
        out_shape=(shape, shape),
        in_specs=[anywhere] * 5,
        out_specs=(vmem, vmem),
        scratch_shapes=[
            pltpu.VMEM(displacements.shape, BF16),
            pltpu.VMEM(material_ids.shape, jnp.int32),
            pltpu.SMEM(lame.shape, F32),
            pltpu.SMEM(slab_bounds.shape, jnp.int32),
            pltpu.VMEM(factors.shape, BF16),
            pltpu.SemaphoreType.DMA((5,)),
            pltpu.VMEM((256, 128), F32),
            pltpu.VMEM((slots, 3, 8, 128), BF16),
            pltpu.VMEM((slots, 3, 8, 128), BF16),
            pltpu.VMEM((groups, 5, 3, GROUP, 128), BF16),
            pltpu.VMEM((groups, 5, 3, GROUP, 128), BF16),
            pltpu.VMEM((groups, 24 * GROUP, 128), F32),
            pltpu.VMEM((groups, 5, 3 * GROUP, 128), F32),
            pltpu.VMEM((256, 128), F32),
            pltpu.VMEM((512, 256), BF16),
            pltpu.VMEM((steps, 128), BF16),
            pltpu.VMEM((6, 8 * slots, 128), F32),
            pltpu.VMEM((3, 128, 512), BF16),
            pltpu.VMEM((3, 64, 512), BF16),
            pltpu.SemaphoreType.DMA,
            pltpu.SemaphoreType.DMA((groups,)),
            pltpu.SemaphoreType.DMA((groups, 5)),
            pltpu.SemaphoreType.DMA((groups, 5)),
        ],
        compiler_params=pltpu.CompilerParams(collective_id=0, has_side_effects=True),
    )(displacements, material_ids, lame, slab_bounds, factors)
    return (jnp.sqrt(3.0 * most), spread * (1.0 / 3.0))


def solution(mesh):
    in_specs = (P("case", None, "bx", "by", None), P("bx", "by", None), P(), P(None, "bx"), P())
    out_specs = (P("bx", "by", "case"), P("bx", "by", "case"))
    return jax.shard_map(shards, mesh=mesh, in_specs=in_specs, out_specs=out_specs, check_vma=False)
```

time: 44.1 us -> 37.9 us (0.86)
  the two profiles are of different devices: /device:TPU:4 before, /device:TPU:68 now
where the time goes in v2:
time: 37.9 us; the launch traced here: 37.6 us
  Pallas kernels  35.6 us (94%)
  other arithmetic  1.41 us (4%)
  between operations  0.64 us (2%)
    pallas_call x1, Pallas kernels, shards(): pl.pallas_call(functools.partial(kernel, (0, 1, 3, 2)), out_shape=(shape,...  35.6 us
    sqrt x1, other arithmetic, shards(): return (jnp.sqrt(3.0 * most), spread * (1.0 / 3.0))  1.41 us

profile of v2, /device:TPU:68, one launch (start us, length us, event | category | flops | bytes accessed | tf_op | source)
XLA Modules:
  0.0 37.6 jit_solution(10825606292073578837)
XLA Ops:
  0.6 35.6 %shard_map.68 = (f32[8,8,8]{2,1,0:T(8,128)}, f32[8,8,8]{2,1,0:T(8,128)}) custom-call(bf16[2,3,8,8,256]{4,3,2,1,0:T(8,128)(2,1)} %disp_any.1, s32[8,8,256]{2,1,0:T(8,128)} %mat_any.1, f32[2,8]{1,0:T(2,128)} %lame_any.1, s32[2,8]{1,0:T(2,128)} %bounds_any.1, bf16[64,1024]{1,0:T(8,128)(2,1)} %bitcast.1), custom_call_target="tpu_custom_call" | custom-call | tf_op jit(solution)/shard_map/pallas_call | solution.py:346
  36.2 1.4 %multiply_sqrt_fusion = (f32[8,8,8]{2,1,0:T(8,128)}, f32[8,8,8]{2,1,0:T(8,128)}) fusion(f32[8,8,8]{2,1,0:T(8,128)} %get-tuple-element.4, f32[8,8,8]{2,1,0:T(8,128)} %get-tuple-element.5), kind=kLoop, calls=%fused_computation | loop fusion | flops 1024 | bytes 8192 | tf_op jit(solution)/shard_map/sqrt | solution.py:378

commit v3 on v2

--- a/solution.py
+++ b/solution.py
@@ -373,8 +373,9 @@
             pltpu.SemaphoreType.DMA((groups, 5)),
             pltpu.SemaphoreType.DMA((groups, 5)),
         ],
-        compiler_params=pltpu.CompilerParams(collective_id=0, has_side_effects=True),
-    )(displacements, material_ids, lame, slab_bounds, factors)
+        compiler_params=pltpu.CompilerParams(collective_id=0, has_side_effects=True, vmem_limit_bytes=32768 * 1024),
+
+    )(*[pltpu.with_memory_space_constraint(v, pltpu.MemorySpace.HBM) for v in (displacements, material_ids, lame, slab_bounds, factors)])
     return (jnp.sqrt(3.0 * most), spread * (1.0 / 3.0))
 
 

time: 37.9 us -> 36.4 us (0.960)
  other arithmetic: 1.41 us -> 0.64 us
  Pallas kernels: 35.6 us -> 35 us
    sqrt x1, other arithmetic: 1.41 us -> 0.64 us  [shards(): return (jnp.sqrt(3.0 * most), spread * (1.0 / 3.0))]
    pallas_call x1, Pallas kernels: 35.6 us -> 35 us  [shards(): pl.pallas_call(functools.partial(kernel, (0, 1, 3, 2)), out_shape=(shape,...]
where the time goes in v3:
time: 36.4 us; the launch traced here: 36.3 us
  Pallas kernels  35 us (96%)
  other arithmetic  0.64 us (2%)
  between operations  0.64 us (2%)
    pallas_call x1, Pallas kernels, shards(): pl.pallas_call(functools.partial(kernel, (0, 1, 3, 2)), out_shape=(shape,...  35 us

profile of v3, /device:TPU:68, one launch (start us, length us, event | category | flops | bytes accessed | tf_op | source)
XLA Modules:
  0.0 36.3 jit_solution(11311124773482474065)
XLA Ops:
  0.6 35.0 %shard_map.68 = (f32[8,8,8]{2,1,0:T(8,128)S(1)}, f32[8,8,8]{2,1,0:T(8,128)S(1)}) custom-call(bf16[2,3,8,8,256]{4,3,2,1,0:T(8,128)(2,1)} %disp_any.1, s32[8,8,256]{2,1,0:T(8,128)} %mat_any.1, f32[2,8]{1,0:T(2,128)} %lame_any.1, s32[2,8]{1,0:T(2,128)} %bounds_any.1, bf16[64,1024]{1,0:T(8,128)(2,1)} %bitcast.1), custom_call_target="tpu_custom_call" | custom-call | tf_op jit(solution)/shard_map/pallas_call | solution.py:346
  35.6 0.6 %multiply_sqrt_fusion = (f32[8,8,8]{2,1,0:T(8,128)}, f32[8,8,8]{2,1,0:T(8,128)}) fusion(f32[8,8,8]{2,1,0:T(8,128)S(1)} %get-tuple-element.4, f32[8,8,8]{2,1,0:T(8,128)S(1)} %get-tuple-element.5), kind=kLoop, calls=%fused_computation | loop fusion | flops 1024 | bytes 8192 | tf_op jit(solution)/shard_map/sqrt | solution.py:379

commit v4 on v3

--- a/solution.py
+++ b/solution.py
@@ -12,12 +12,14 @@
 F32 = jnp.float32
 BF16 = jnp.bfloat16
 GROUP = 8
+BLOCK = 256
 
 
 def kernel(
     order, disp_any, mat_any, lame_any, bounds_any, hist_any, most_ref, spread_ref,
     disp_ref, mat_ref, lame_ref, bounds_ref, hist_ref, loaded,
-    turned, send, own, faces, halos, rows_ref, halo_rows, moduli, weights, factors, cells, rhs, rhs_shear,
+    turned, send, own, faces, halos, rows_ref, halo_rows, moduli, weights, factors, cells,
+    rhs_in, shear_in, rhs_two, shear_two, rhs_out, shear_out, factors_two, factors_shear,
     sent, got, face_sent, face_got,
 ):
     case = lax.axis_index("case")
@@ -28,6 +30,12 @@
     x_next = {"bx": lax.rem(bx + 1, bricks)}
     x_prev = {"bx": lax.rem(bx + bricks - 1, bricks)}
     partner = {"by": 1 - by}
+    groups = slots // GROUP
+    group = case // GROUP
+
+    def relative(source, target):
+        return lax.rem(source - target + groups, groups)
+
     above = {"case": lax.rem(case + 1, slots)}
     below = {"case": lax.rem(case + slots - 1, slots)}
 
@@ -62,16 +70,17 @@
         send[:, a] = turned[...].reshape(slots, 8, 128).astype(BF16)
 
     pl.semaphore_wait(barrier, slots + 2)
-    mine = pltpu.make_async_copy(send.at[case], own.at[case], got.at[case // GROUP])
+    mine = pltpu.make_async_copy(send.at[case], own.at[lax.rem(case, GROUP)], got.at[0])
     mine.start()
     for target in range(slots):
         @pl.when(target != case)
         def _():
+            place = relative(group, target // GROUP)
             pltpu.make_async_remote_copy(
                 src_ref=send.at[target],
-                dst_ref=own.at[case],
+                dst_ref=own.at[place * GROUP + lax.rem(case, GROUP)],
                 send_sem=sent,
-                recv_sem=got.at[case // GROUP],
+                recv_sem=got.at[place],
                 device_id={"case": target},
                 device_id_type=MESH,
             ).start()
@@ -79,13 +88,23 @@
     loads[1].wait()
     r = lax.broadcasted_iota(jnp.int32, (64, 128), 0)
     c = lax.broadcasted_iota(jnp.int32, (64, 128), 1)
-    permute = (r == 2 * (c % slots) + (c // slots) % 2).astype(F32).astype(BF16)
+    source = (c // (2 * GROUP) + group) % groups * GROUP + c % GROUP
+    permute = (r == 2 * source + (c // GROUP) % 2).astype(F32).astype(BF16)
     steps = hist_ref.shape[1]
     for begin in range(0, steps, 256):
         block = hist_ref[:, begin : begin + 256].astype(F32).T.astype(BF16)
         factors[begin : begin + 256, :] = jnp.dot(
             block, permute, preferred_element_type=F32
         ).astype(BF16)
+
+    half = steps // 2
+    near = lax.broadcasted_iota(jnp.int32, (half, 128), 1) < 64
+    early, late = factors[0:half, :], factors[half:steps, :]
+    factors_two[:, 0:128] = early
+    factors_two[:, 128:256] = late
+    factors_shear[...] = jnp.where(near, early.astype(F32), late.astype(F32)).astype(BF16)
+    rhs_two[...] = jnp.zeros(rhs_two.shape, BF16)
+    shear_two[...] = jnp.zeros(shear_two.shape, BF16)
 
     for load in loads[2:]:
         load.wait()
@@ -127,13 +146,12 @@
     none = jnp.zeros((128, 128), BF16)
     weights[0:128, 0:128] = picked((r == c + 8) & (cx < 7), (r == c - 8) & (cx > 0))
     weights[0:128, 128:256] = picked((r == c + 1) & (cy < 7), (r == c - 1) & (cy > 0))
-    weights[128:256, 0:128] = picked(never, same & (r % 8 == cy) & (cx == 0) & has_low)
-    weights[256:384, 0:128] = picked(same & (r % 8 == cy) & (cx == 7) & has_high, never)
-    weights[128:256, 128:256] = none
-    weights[256:384, 128:256] = none
-    weights[384:512, 0:128] = none
     alike = same & ((r // 8) % 8 == cx)
-    weights[384:512, 128:256] = picked(alike & (cy == 7) & lower, alike & (cy == 0) & upper)
+    weights[128:256, 0:128] = none
+    weights[128:256, 128:256] = picked(alike & (cy == 7) & lower, alike & (cy == 0) & upper)
+    weights[256:384, 0:128] = picked(never, same & (r % 8 == cy) & (cx == 0) & has_low)
+    weights[384:512, 0:128] = picked(same & (r % 8 == cy) & (cx == 7) & has_high, never)
+    weights[256:512, 128:256] = jnp.zeros((256, 128), BF16)
 
     in_upper = jnp.full((GROUP, 128), by, jnp.int32) > 0
     moves = {}
@@ -173,11 +191,14 @@
         for k, target in enumerate((x_next, x_prev, partner, above, below)):
             for a in range(3):
                 faces[g, k, a] = packed[k][a].astype(BF16)
+            place = g
+            if k >= 3:
+                place = lax.rem(g + relative(group, target["case"] // GROUP), groups)
             move = pltpu.make_async_remote_copy(
                 src_ref=faces.at[g, k],
-                dst_ref=halos.at[g, k],
+                dst_ref=halos.at[place, k],
                 send_sem=face_sent.at[g, k],
-                recv_sem=face_got.at[g, k],
+                recv_sem=face_got.at[place, k],
                 device_id=target,
                 device_id_type=MESH,
             )
@@ -191,23 +212,29 @@
 
     in_column = column == row
     in_row = lane % 8 == row
-    for g in order:
-        s0 = GROUP * g
-        for k in range(5):
+    left = lane < 64
+
+    def fetch(g, kinds):
+        for k in kinds:
+            arrival = pltpu.make_async_remote_copy(
+                src_ref=faces.at[g, k], dst_ref=halos.at[g, k], send_sem=face_sent.at[g, k],
+                recv_sem=face_got.at[g, k], device_id=partner, device_id_type=MESH,
+            ).wait_recv
             if k < 3:
-                moves[g, k].wait_recv()
+                arrival()
             elif k == 3:
-                pl.when(case > 0)(moves[g, k].wait_recv)
+                pl.when(case > 0)(arrival)
             else:
-                pl.when(case < slots - 1)(moves[g, k].wait_recv)
+                pl.when(case < slots - 1)(arrival)
             halo_rows[g, k] = halos[g, k].astype(F32).reshape(3 * GROUP, 128)
 
+    def stresses(g, full):
         def halo(k, i, a):
             at = GROUP * a + i
             return jnp.broadcast_to(halo_rows[g, k, at : at + 1, :], (8, 128))
 
         parts = [rows_ref[g]]
-        for k, mask in ((0, in_column), (1, in_column), (2, in_row)):
+        for k, mask in ((2, in_row), (0, in_column), (1, in_column))[: 3 if full else 1]:
             parts.append(
                 jnp.concatenate(
                     [
@@ -219,22 +246,17 @@
                 )
             )
         flat = jnp.concatenate([part.astype(BF16) for part in parts], axis=1)
-        planar = jnp.dot(flat, weights[...], preferred_element_type=F32)
+        planar = jnp.dot(flat, weights[0 : flat.shape[1], :], preferred_element_type=F32)
         for i in range(GROUP):
             grads = []
             for a in range(3):
                 at = 24 * i + 8 * a
                 field = rows_ref[g, at : at + 8]
-                down = jnp.where(
-                    row == 0,
-                    halo(3, i, a),
-                    pltpu.roll(field, 1, 0),
-                )
-                up = jnp.where(
-                    row == 7,
-                    halo(4, i, a),
-                    pltpu.roll(field, 7, 0),
-                )
+                down = pltpu.roll(field, 1, 0)
+                up = pltpu.roll(field, 7, 0)
+                if full:
+                    down = jnp.where(row == 0, halo(3, i, a), down)
+                    up = jnp.where(row == 7, halo(4, i, a), up)
                 grads.append(
                     (planar[at : at + 8, 0:128], planar[at : at + 8, 128:256], 0.5 * (up - down))
                 )
@@ -260,42 +282,68 @@
                 s_zx,
             )
             for k in range(6):
-                cells[k, pl.ds(s0 + i, 8, stride=slots), :] = values[k]
-
-    left = lax.broadcasted_iota(jnp.int32, (slots, 128), 1) < 64
-    for k in range(6):
-        for p in range(4):
-            even = cells[k, 2 * p * slots : (2 * p + 1) * slots]
-            odd = cells[k, (2 * p + 1) * slots : (2 * p + 2) * slots]
-            first = jnp.where(left, even, pltpu.roll(odd, 64, 1))
-            second = jnp.where(left, pltpu.roll(even, 64, 1), odd)
-            both = jnp.concatenate([first, second], axis=0)
-            coarse = both.astype(BF16)
+                cells[g, k, pl.ds(i, 8, stride=GROUP), :] = values[k]
+
+    def level_of(g, k, z):
+        return cells[g, k, GROUP * z : GROUP * (z + 1)]
+
+    def keep(g, k, first, second, normal_ref, shear_ref, spots):
+        both = jnp.concatenate([first, second], axis=0)
+        coarse = both.astype(BF16)
+        fine = (both - coarse.astype(F32)).astype(BF16)
+        rows_here = 2 * GROUP
+        for down, at in spots:
+            begin = rows_here * g + down * (2 if k < 3 else 1)
             if k < 3:
-                fine = (both - coarse.astype(F32)).astype(BF16)
-                rhs[k, 0:64, 128 * p : 128 * (p + 1)] = coarse
-                rhs[k, 64:128, 128 * p : 128 * (p + 1)] = fine
+                normal_ref[k, begin : begin + rows_here, at : at + 128] = coarse
+                normal_ref[k, 64 + begin : 64 + begin + rows_here, at : at + 128] = fine
             else:
-                rhs_shear[k - 3, :, 128 * p : 128 * (p + 1)] = coarse
-
-    block = 256
-    results = []
-    for n in range(2):
-        columns = slice(256 * n, 256 * (n + 1))
+                shear_ref[k - 3, begin : begin + rows_here, at : at + 128] = coarse
+
+    def pair_up(g, k, z_first, z_second, normal_ref, shear_ref, spots):
+        one, two = level_of(g, k, z_first), level_of(g, k, z_second)
+        first = jnp.where(left, one, pltpu.roll(two, 64, 1))
+        second = jnp.where(left, pltpu.roll(one, 64, 1), two)
+        keep(g, k, first, second, normal_ref, shear_ref, spots)
+
+    def inner_columns(g):
+        for k in range(6):
+            pair_up(g, k, 1, 2, rhs_in, shear_in, ((0, 0),))
+            pair_up(g, k, 3, 4, rhs_in, shear_in, ((0, 128),))
+            pair_up(g, k, 5, 6, rhs_two, shear_two, ((0, 0), (64, 128)))
+
+    def outer_columns(g):
+        for k in range(6):
+            pair_up(g, k, 0, 7, rhs_out, shear_out, ((0, 0),))
+            first = second = jnp.zeros((GROUP, 128), F32)
+            for z in range(1, 7):
+                one = level_of(g, k, z)
+                for side in range(2):
+                    here = lane // 8 == 8 * side + z
+                    turn = 8 * z + 8 * side
+                    first = jnp.where(here, pltpu.roll(one, turn % 128, 1), first)
+                    second = jnp.where(here, pltpu.roll(one, (turn - 64) % 128, 1), second)
+            keep(g, k, first, second, rhs_out, shear_out, ((0, 128),))
+
+    def extremes(lhs_ref, lhs_shear_ref, normal_ref, shear_ref):
+        width = 256
+        deep = shear_ref.shape[1]
 
         def body(i, carry):
             most, upper_h, lower_h = carry
-            full = factors[pl.ds(pl.multiple_of(i * block, block), block), :]
+            here = pl.ds(pl.multiple_of(i * BLOCK, BLOCK), BLOCK)
+            full = lhs_ref[here, :]
+            thin = lhs_shear_ref[here, 0:deep]
             total = None
             for k in (0, 1):
-                part = jnp.dot(full, rhs[k, :, columns], preferred_element_type=F32)
+                part = jnp.dot(full, normal_ref[k], preferred_element_type=F32)
                 total = part * part if total is None else total + part * part
             for k in range(3):
-                part = jnp.dot(full[:, 0:64], rhs_shear[k, :, columns], preferred_element_type=F32)
+                part = jnp.dot(thin, shear_ref[k], preferred_element_type=F32)
                 total = total + part * part
-            mean = jnp.dot(full, rhs[2, :, columns], preferred_element_type=F32)
-            total = total.reshape(block // 8, 8, 256)
-            mean = mean.reshape(block // 8, 8, 256)
+            mean = jnp.dot(full, normal_ref[2], preferred_element_type=F32)
+            total = total.reshape(BLOCK // 8, 8, width)
+            mean = mean.reshape(BLOCK // 8, 8, width)
             return (
                 jnp.maximum(most, jnp.max(total, axis=0)),
                 jnp.maximum(upper_h, jnp.max(mean, axis=0)),
@@ -303,22 +351,51 @@
             )
 
         start = (
-            jnp.zeros((8, 256), F32),
-            jnp.full((8, 256), -jnp.inf, F32),
-            jnp.full((8, 256), jnp.inf, F32),
+            jnp.zeros((8, width), F32),
+            jnp.full((8, width), -jnp.inf, F32),
+            jnp.full((8, width), jnp.inf, F32),
         )
-        most, upper_h, lower_h = lax.fori_loop(0, steps // block, body, start)
+        most, upper_h, lower_h = lax.fori_loop(0, lhs_ref.shape[0] // BLOCK, body, start)
         most = jnp.max(most, axis=0, keepdims=True)
         upper_h = jnp.max(upper_h, axis=0, keepdims=True)
         lower_h = jnp.min(lower_h, axis=0, keepdims=True)
-        results.append((most, upper_h - lower_h))
-
+        return (most, upper_h, lower_h)
+
+    for g in order:
+        fetch(g, (2,))
+        stresses(g, False)
+        inner_columns(g)
+    most, upper_h, lower_h = extremes(factors, factors, rhs_in, shear_in)
+    inner = [(most, upper_h - lower_h)]
+    most, upper_h, lower_h = extremes(factors_two, factors_shear, rhs_two, shear_two)
+    inner.append(
+        (
+            jnp.maximum(most[:, 0:128], most[:, 128:256]),
+            jnp.maximum(upper_h[:, 0:128], upper_h[:, 128:256])
+            - jnp.minimum(lower_h[:, 0:128], lower_h[:, 128:256]),
+        )
+    )
+    for g in order:
+        fetch(g, (0, 1, 3, 4))
+        stresses(g, True)
+        outer_columns(g)
+    most, upper_h, lower_h = extremes(factors, factors, rhs_out, shear_out)
+    outer = (most, upper_h - lower_h)
+
+    spot = lax.broadcasted_iota(jnp.int32, (1, 128), 1)
     for which, out_ref in ((0, most_ref), (1, spread_ref)):
-        rows = []
-        for n in range(2):
-            for p in range(2):
-                pair_row = results[n][which][:, 128 * p : 128 * (p + 1)]
-                rows += [pair_row, pltpu.roll(pair_row, 64, 1)]
+        ends = outer[which][:, 0:128]
+        sides = outer[which][:, 128:256]
+        pairs = [inner[0][which][:, 0:128], inner[0][which][:, 128:256], inner[1][which]]
+        rows = [ends]
+        for z in range(1, 7):
+            line = pairs[(z - 1) // 2]
+            if z % 2 == 0:
+                line = pltpu.roll(line, 64, 1)
+            line = jnp.where(spot < 8, pltpu.roll(sides, -8 * z % 128, 1), line)
+            line = jnp.where(spot >= 56, pltpu.roll(sides, (-8 * z - 8) % 128, 1), line)
+            rows.append(line)
+        rows.append(pltpu.roll(ends, 64, 1))
         out_ref[...] = jnp.concatenate(rows, axis=0).T[0:64].reshape(8, 8, 8)
 
     whole = send.at[pl.ds(0, slots - 1)]
@@ -365,9 +442,15 @@
             pltpu.VMEM((256, 128), F32),
             pltpu.VMEM((512, 256), BF16),
             pltpu.VMEM((steps, 128), BF16),
-            pltpu.VMEM((6, 8 * slots, 128), F32),
-            pltpu.VMEM((3, 128, 512), BF16),
-            pltpu.VMEM((3, 64, 512), BF16),
+            pltpu.VMEM((groups, 6, 8 * GROUP, 128), F32),
+            pltpu.VMEM((3, 128, 256), BF16),
+            pltpu.VMEM((3, 64, 256), BF16),
+            pltpu.VMEM((3, 256, 256), BF16),
+            pltpu.VMEM((3, 128, 256), BF16),
+            pltpu.VMEM((3, 128, 256), BF16),
+            pltpu.VMEM((3, 64, 256), BF16),
+            pltpu.VMEM((steps // 2, 256), BF16),
+            pltpu.VMEM((steps // 2, 128), BF16),
             pltpu.SemaphoreType.DMA,
             pltpu.SemaphoreType.DMA((groups,)),
             pltpu.SemaphoreType.DMA((groups, 5)),

time: 36.4 us -> 35.2 us (0.967)
  the two profiles are of different devices: /device:TPU:68 before, /device:TPU:1 now
where the time goes in v4:
time: 35.2 us; the launch traced here: 35 us
  Pallas kernels  33.8 us (96%)
  other arithmetic  0.64 us (2%)
  between operations  0.64 us (2%)
    pallas_call x1, Pallas kernels, shards(): pl.pallas_call(functools.partial(kernel, (0, 1, 3, 2)), out_shape=(shape,...  33.8 us

profile of v4, /device:TPU:1, one launch (start us, length us, event | category | flops | bytes accessed | tf_op | source)
XLA Modules:
  0.0 35.0 jit_solution(13707387254324675170)
XLA Ops:
  0.6 33.8 %shard_map.68 = (f32[8,8,8]{2,1,0:T(8,128)S(1)}, f32[8,8,8]{2,1,0:T(8,128)S(1)}) custom-call(bf16[2,3,8,8,256]{4,3,2,1,0:T(8,128)(2,1)} %disp_any.1, s32[8,8,256]{2,1,0:T(8,128)} %mat_any.1, f32[2,8]{1,0:T(2,128)} %lame_any.1, s32[2,8]{1,0:T(2,128)} %bounds_any.1, bf16[64,1024]{1,0:T(8,128)(2,1)} %bitcast.1), custom_call_target="tpu_custom_call" | custom-call | tf_op jit(solution)/shard_map/pallas_call | solution.py:423
  34.4 0.6 %multiply_sqrt_fusion = (f32[8,8,8]{2,1,0:T(8,128)}, f32[8,8,8]{2,1,0:T(8,128)}) fusion(f32[8,8,8]{2,1,0:T(8,128)S(1)} %get-tuple-element.4, f32[8,8,8]{2,1,0:T(8,128)S(1)} %get-tuple-element.5), kind=kLoop, calls=%fused_computation | loop fusion | flops 1024 | bytes 8192 | tf_op jit(solution)/shard_map/sqrt | solution.py:462

commit v5 on v4

--- a/solution.py
+++ b/solution.py
@@ -12,7 +12,7 @@
 F32 = jnp.float32
 BF16 = jnp.bfloat16
 GROUP = 8
-BLOCK = 256
+BLOCK = 1024
 
 
 def kernel(
@@ -328,10 +328,11 @@
     def extremes(lhs_ref, lhs_shear_ref, normal_ref, shear_ref):
         width = 256
         deep = shear_ref.shape[1]
+        block = min(BLOCK, lhs_ref.shape[0])
 
         def body(i, carry):
             most, upper_h, lower_h = carry
-            here = pl.ds(pl.multiple_of(i * BLOCK, BLOCK), BLOCK)
+            here = pl.ds(pl.multiple_of(i * block, block), block)
             full = lhs_ref[here, :]
             thin = lhs_shear_ref[here, 0:deep]
             total = None
@@ -342,8 +343,8 @@
                 part = jnp.dot(thin, shear_ref[k], preferred_element_type=F32)
                 total = total + part * part
             mean = jnp.dot(full, normal_ref[2], preferred_element_type=F32)
-            total = total.reshape(BLOCK // 8, 8, width)
-            mean = mean.reshape(BLOCK // 8, 8, width)
+            total = total.reshape(block // 8, 8, width)
+            mean = mean.reshape(block // 8, 8, width)
             return (
                 jnp.maximum(most, jnp.max(total, axis=0)),
                 jnp.maximum(upper_h, jnp.max(mean, axis=0)),
@@ -355,7 +356,7 @@
             jnp.full((8, width), -jnp.inf, F32),
             jnp.full((8, width), jnp.inf, F32),
         )
-        most, upper_h, lower_h = lax.fori_loop(0, lhs_ref.shape[0] // BLOCK, body, start)
+        most, upper_h, lower_h = lax.fori_loop(0, lhs_ref.shape[0] // block, body, start)
         most = jnp.max(most, axis=0, keepdims=True)
         upper_h = jnp.max(upper_h, axis=0, keepdims=True)
         lower_h = jnp.min(lower_h, axis=0, keepdims=True)

time: 35.2 us -> 34.5 us (0.980)
  the two profiles are of different devices: /device:TPU:1 before, /device:TPU:68 now
where the time goes in v5:
time: 34.5 us; the launch traced here: 34.4 us
  Pallas kernels  33.1 us (96%)
  other arithmetic  0.64 us (2%)
  between operations  0.64 us (2%)
    pallas_call x1, Pallas kernels, shards(): pl.pallas_call(functools.partial(kernel, (0, 1, 3, 2)), out_shape=(shape,...  33.1 us

profile of v5, /device:TPU:68, one launch (start us, length us, event | category | flops | bytes accessed | tf_op | source)
XLA Modules:
  0.0 34.4 jit_solution(12845302621913679039)
XLA Ops:
  0.6 33.1 %shard_map.68 = (f32[8,8,8]{2,1,0:T(8,128)S(1)}, f32[8,8,8]{2,1,0:T(8,128)S(1)}) custom-call(bf16[2,3,8,8,256]{4,3,2,1,0:T(8,128)(2,1)} %disp_any.1, s32[8,8,256]{2,1,0:T(8,128)} %mat_any.1, f32[2,8]{1,0:T(2,128)} %lame_any.1, s32[2,8]{1,0:T(2,128)} %bounds_any.1, bf16[64,1024]{1,0:T(8,128)(2,1)} %bitcast.1), custom_call_target="tpu_custom_call" | custom-call | tf_op jit(solution)/shard_map/pallas_call | solution.py:424
  33.7 0.6 %multiply_sqrt_fusion = (f32[8,8,8]{2,1,0:T(8,128)}, f32[8,8,8]{2,1,0:T(8,128)}) fusion(f32[8,8,8]{2,1,0:T(8,128)S(1)} %get-tuple-element.4, f32[8,8,8]{2,1,0:T(8,128)S(1)} %get-tuple-element.5), kind=kLoop, calls=%fused_computation | loop fusion | flops 1024 | bytes 8192 | tf_op jit(solution)/shard_map/sqrt | solution.py:463

commit v6 on v5

--- a/solution.py
+++ b/solution.py
@@ -172,25 +172,28 @@
             device_id=partner, device_id_type=MESH,
         ).wait_recv()
         rows_ref[g] = own[s0 : s0 + GROUP].astype(F32).reshape(24 * GROUP, 128)
-        packed = [[], [], [], [], []]
-        for a in range(3):
-            to_next = to_prev = to_side = jnp.zeros((GROUP, 128), F32)
-            for z in range(8):
-                value = rows_ref[g, pl.ds(8 * a + z, GROUP, stride=24), :]
-                to_next = jnp.where(column == z, pltpu.roll(value, (8 * z - 56) % 128, 1), to_next)
-                to_prev = jnp.where(column == z, pltpu.roll(value, 8 * z, 1), to_prev)
-                turn = jnp.where(in_upper, pltpu.roll(value, z, 1), pltpu.roll(value, (z - 7) % 128, 1))
-                to_side = jnp.where(lane % 8 == z, turn, to_side)
-                if z == 0:
-                    packed[4].append(value)
-                if z == 7:
-                    packed[3].append(value)
-            packed[0].append(to_next)
-            packed[1].append(to_prev)
-            packed[2].append(to_side)
-        for k, target in enumerate((x_next, x_prev, partner, above, below)):
+        values = [
+            [rows_ref[g, pl.ds(8 * a + z, GROUP, stride=24), :] for z in range(8)] for a in range(3)
+        ]
+
+        def face(k, a):
+            if k >= 3:
+                return values[a][7 if k == 3 else 0]
+            total = jnp.zeros((GROUP, 128), F32)
+            for z, value in enumerate(values[a]):
+                if k == 2:
+                    turn = jnp.where(
+                        in_upper, pltpu.roll(value, z, 1), pltpu.roll(value, (z - 7) % 128, 1)
+                    )
+                    total = jnp.where(lane % 8 == z, turn, total)
+                else:
+                    turn = pltpu.roll(value, (8 * z - 56 * (1 - k)) % 128, 1)
+                    total = jnp.where(column == z, turn, total)
+            return total
+
+        for k, target in ((3, above), (4, below), (0, x_next), (1, x_prev), (2, partner)):
             for a in range(3):
-                faces[g, k, a] = packed[k][a].astype(BF16)
+                faces[g, k, a] = face(k, a).astype(BF16)
             place = g
             if k >= 3:
                 place = lax.rem(g + relative(group, target["case"] // GROUP), groups)

time: 34.5 us -> 34.5 us (level)
  no operation moved by 1% of the time
where the time goes in v6:
time: 34.5 us; the launch traced here: 34.4 us
  Pallas kernels  33.1 us (96%)
  other arithmetic  0.64 us (2%)
  between operations  0.64 us (2%)
    pallas_call x1, Pallas kernels, shards(): pl.pallas_call(functools.partial(kernel, (0, 1, 3, 2)), out_shape=(shape,...  33.1 us

profile of v6, /device:TPU:68, one launch (start us, length us, event | category | flops | bytes accessed | tf_op | source)
XLA Modules:
  0.0 34.4 jit_solution(1483920376805735538)
XLA Ops:
  0.6 33.1 %shard_map.68 = (f32[8,8,8]{2,1,0:T(8,128)S(1)}, f32[8,8,8]{2,1,0:T(8,128)S(1)}) custom-call(bf16[2,3,8,8,256]{4,3,2,1,0:T(8,128)(2,1)} %disp_any.1, s32[8,8,256]{2,1,0:T(8,128)} %mat_any.1, f32[2,8]{1,0:T(2,128)} %lame_any.1, s32[2,8]{1,0:T(2,128)} %bounds_any.1, bf16[64,1024]{1,0:T(8,128)(2,1)} %bitcast.1), custom_call_target="tpu_custom_call" | custom-call | tf_op jit(solution)/shard_map/pallas_call | solution.py:427
  33.7 0.6 %multiply_sqrt_fusion = (f32[8,8,8]{2,1,0:T(8,128)}, f32[8,8,8]{2,1,0:T(8,128)}) fusion(f32[8,8,8]{2,1,0:T(8,128)S(1)} %get-tuple-element.4, f32[8,8,8]{2,1,0:T(8,128)S(1)} %get-tuple-element.5), kind=kLoop, calls=%fused_computation | loop fusion | flops 1024 | bytes 8192 | tf_op jit(solution)/shard_map/sqrt | solution.py:466
